TPU v7x, 128 devices: a whole 4x4x4 slice. The times are simulated.
128 devices in a mesh: row: 8 (over z, core), col: 16 (over y, x).
Axes of the slice: x: 4, y: 4, z: 4, core: 2. Of those that a mesh axis runs over, the one named last changes fastest.
Arguments:
- kernel: float32 [16384, 16384], P('row', 'col'), may hold values from 0 to 3, as said below
Outputs:
- trailing: float32 [16384, 16384], P('row', 'col')
- factor_t: float32 [1024, 16384], P('col', 'row')
Inputs may be any that keep to these rules, and one draw needn't show every extreme that they name: K is symmetric: an RBF kernel over 256 donor features plus each donor's noise variance, of 0.5 or more, on the diagonal.
All inputs are finite; a program needn't handle non-finite values.
Results may differ from a plain program's by a relative error of at most 0.0003.
Values sent between devices are 32-bit elements; how exact they have to be, the bound alone decides.
A program may use at most 128 MiB of HBM per device.

v0:
```python
import jax
import jax.numpy as jnp
from jax import lax
from jax.sharding import PartitionSpec as P

PANEL = 512
PANELS = 2


def from_root(value, axis, source):
    kept = jnp.where(lax.axis_index(axis) == source, value, 0).astype(value.dtype)
    return lax.psum(kept, axis)


def outer_update(left_fac, right_fac):
    return lax.dot_general(
        left_fac,
        right_fac,
        (((0,), (0,)), ((), ())),
        precision=lax.Precision.HIGHEST,
        preferred_element_type=jnp.float32,
    )


def local(kernel):
    grid_rows = lax.axis_size("row")
    grid_cols = lax.axis_size("col")
    my_row = lax.axis_index("row")
    my_col = lax.axis_index("col")
    rows_loc = kernel.shape[0]
    cols_loc = kernel.shape[1]
    tile_w = PANEL // grid_cols
    spread = grid_cols // grid_rows
    row_local = jnp.arange(rows_loc, dtype=jnp.int32)
    row_ids = (row_local // tile_w * grid_rows + my_row) * tile_w + row_local % tile_w
    col_local = jnp.arange(cols_loc, dtype=jnp.int32)
    col_ids = (col_local // tile_w * grid_cols + my_col) * tile_w + col_local % tile_w
    down_list = []
    schur = kernel
    for panel_idx in range(PANELS):
        column_tile = schur[:, panel_idx * tile_w : (panel_idx + 1) * tile_w]
        first_col = panel_idx * PANEL
        first_tile = panel_idx * spread
        corner = column_tile[first_tile * tile_w : (first_tile + spread) * tile_w]
        flat_block = corner.reshape(1, spread * tile_w * tile_w)
        blocks = lax.all_gather(flat_block, ("row", "col"), axis=0, tiled=True)
        blocks = blocks.reshape(grid_rows, grid_cols, spread, tile_w, tile_w)
        blocks = blocks.transpose(2, 0, 3, 1, 4).reshape(PANEL, PANEL)
        lower_fac = jnp.linalg.cholesky(blocks)
        columns_t = column_tile.T
        gathered = lax.all_gather(columns_t, "col", axis=0, tiled=True)
        factor_loc = jax.scipy.linalg.solve_triangular(lower_fac, gathered, lower=True)
        factor_loc = jnp.where(row_ids[None, :] >= first_col, factor_loc, 0.0)
        picked = factor_loc.reshape(PANEL, cols_loc // tile_w, spread, tile_w)
        picked = lax.dynamic_index_in_dim(picked, my_col // grid_rows, 2, keepdims=False)
        picked = picked.reshape(PANEL, cols_loc)
        across = from_root(picked, "row", my_col % grid_rows)
        factor_loc, across = (factor_loc, across)
        schur = schur - outer_update(factor_loc, across)
        down_list.append(factor_loc)
    limit = PANELS * PANEL
    keep = (row_ids[:, None] >= limit) & (col_ids[None, :] >= limit)
    trailing = jnp.where(keep, schur, 0.0)
    stacked = jnp.concatenate(down_list, axis=0)
    per_col = PANELS * PANEL // grid_cols
    factor_out = lax.dynamic_slice_in_dim(stacked, my_col * per_col, per_col, 0)
    return (trailing, factor_out)


def solution(mesh):
    return jax.shard_map(
        local,
        mesh=mesh,
        in_specs=(P("row", "col"),),
        out_specs=(P("row", "col"), P("col", "row")),
        check_vma=False,
    )
```

profile of v0, /device:TPU:0, one launch (start us, length us, event | category | flops | bytes accessed | tf_op | source)
XLA Modules:
  0.0 662.9 jit_solution(6436545868017596230)
XLA Ops:
  8.7 9.1 %copy.22 = f32[2048,1024]{0,1:T(8,128)} copy(f32[2048,1024]{1,0:T(8,128)} %param.4) | data formatting | bytes 16777216 | tf_op args[0]
  19.7 57.2 %all-gather.11.cloned.1.call-done = f32[128,1,2048]{2,1,0:T(1,128)} async-done(((f32[1,1,2048]{2,1,0:T(1,128)}), f32[128,1,2048]{2,1,0:T(1,128)}) %all-gather.11.cloned.1.call-update) | async-done | bytes 1048592 | tf_op jit(solution)/shard_map/all_gather | solution.py:46
  93.2 11.7 %cholesky.286 = f32[128,128]{1,0:T(8,128)S(1)} custom-call(f32[128,128]{1,0:T(8,128)S(1)} %cholesky.426), custom_call_target="Cholesky" | custom-call | tf_op jit(solution)/shard_map/jit(cholesky)/cholesky | solution.py:49
  105.0 9.8 %custom-call.27 = f32[1,128,128]{1,2,0:T(8,128)S(1)} custom-call(f32[1,128,128]{2,1,0:T(8,128)S(1)} %get-tuple-element.65), custom_call_target="InvertDiagBlocksLowerTriangular" | custom-call | tf_op jit(solution)/shard_map/jit(cholesky)/cholesky | solution.py:49
  115.6 11.7 %cholesky.305 = f32[128,128]{1,0:T(8,128)S(1)} custom-call(f32[128,128]{1,0:T(8,128)S(1)} %cholesky.430), custom_call_target="Cholesky" | custom-call | tf_op jit(solution)/shard_map/jit(cholesky)/cholesky | solution.py:49
  127.3 10.0 %custom-call.28 = f32[1,128,128]{1,2,0:T(8,128)S(1)} custom-call(f32[1,128,128]{2,1,0:T(8,128)S(1)} %get-tuple-element.62), custom_call_target="InvertDiagBlocksLowerTriangular" | custom-call | tf_op jit(solution)/shard_map/jit(cholesky)/cholesky | solution.py:49
  138.0 11.7 %cholesky.326 = f32[128,128]{1,0:T(8,128)S(1)} custom-call(f32[128,128]{1,0:T(8,128)S(1)} %cholesky.435), custom_call_target="Cholesky" | custom-call | tf_op jit(solution)/shard_map/jit(cholesky)/cholesky | solution.py:49
  149.7 9.8 %custom-call.29 = f32[1,128,128]{1,2,0:T(8,128)S(1)} custom-call(f32[1,128,128]{2,1,0:T(8,128)S(1)} %get-tuple-element.59), custom_call_target="InvertDiagBlocksLowerTriangular" | custom-call | tf_op jit(solution)/shard_map/jit(cholesky)/cholesky | solution.py:49
  160.2 11.7 %cholesky.343 = f32[128,128]{1,0:T(8,128)S(1)} custom-call(f32[128,128]{1,0:T(8,128)S(1)} %convolution_subtract_fusion.10), custom_call_target="Cholesky" | custom-call | tf_op jit(solution)/shard_map/jit(cholesky)/cholesky | solution.py:49
  184.8 39.3 %custom-call.30 = f32[4,128,128]{1,2,0:T(8,128)S(1)} custom-call(f32[4,128,128]{2,1,0:T(8,128)S(1)} %get-tuple-element.18), custom_call_target="InvertDiagBlocksLowerTriangular" | custom-call | tf_op jit(solution)/shard_map/jit(_solve_triangular)/triangular_solve | solution.py:52
  246.5 63.6 %all-reduce.4.cloned.1.call-done = f32[512,1024]{0,1:T(8,128)} async-done(((f32[512,1024]{0,1:T(8,128)}), f32[512,1024]{0,1:T(8,128)}) %all-reduce.4.cloned.1.call-update) | async-done | bytes 2097168 | tf_op jit(solution)/shard_map/psum | solution.py:12
  310.2 17.0 %convolution_subtract_fusion = f32[2048,1024]{0,1:T(8,128)S(1)} fusion(f32[2048,1024]{0,1:T(8,128)} %copy.22, f32[512,2048]{1,0:T(8,128)} %maximum_select_fusion, f32[512,1024]{0,1:T(8,128)} %all-reduce.4.cloned.1.call-done), kind=kOutput, calls=%fused_computation.9 | convolution fusion | flops 12886999040 | bytes 23068672 | tf_op jit(solution)/shard_map/dot_general | solution.py:16
  333.3 61.3 %all-gather.13.cloned.1.call-done = f32[128,1,2048]{2,1,0:T(1,128)} async-done(((f32[1,1,2048]{2,1,0:T(1,128)}), f32[128,1,2048]{2,1,0:T(1,128)}) %all-gather.13.cloned.1.call-update) | async-done | bytes 1048592 | tf_op jit(solution)/shard_map/all_gather | solution.py:46
  411.0 11.7 %cholesky.358 = f32[128,128]{1,0:T(8,128)S(1)} custom-call(f32[128,128]{1,0:T(8,128)S(1)} %cholesky.439), custom_call_target="Cholesky" | custom-call | tf_op jit(solution)/shard_map/jit(cholesky)/cholesky | solution.py:49
  422.8 9.8 %custom-call.31 = f32[1,128,128]{1,2,0:T(8,128)S(1)} custom-call(f32[1,128,128]{2,1,0:T(8,128)S(1)} %get-tuple-element.55), custom_call_target="InvertDiagBlocksLowerTriangular" | custom-call | tf_op jit(solution)/shard_map/jit(cholesky)/cholesky | solution.py:49
  433.3 11.7 %cholesky.377 = f32[128,128]{1,0:T(8,128)S(1)} custom-call(f32[128,128]{1,0:T(8,128)S(1)} %cholesky.443), custom_call_target="Cholesky" | custom-call | tf_op jit(solution)/shard_map/jit(cholesky)/cholesky | solution.py:49
  445.1 10.2 %custom-call.32 = f32[1,128,128]{1,2,0:T(8,128)S(1)} custom-call(f32[1,128,128]{2,1,0:T(8,128)S(1)} %get-tuple-element.52), custom_call_target="InvertDiagBlocksLowerTriangular" | custom-call | tf_op jit(solution)/shard_map/jit(cholesky)/cholesky | solution.py:49
  455.9 11.7 %cholesky.398 = f32[128,128]{1,0:T(8,128)S(1)} custom-call(f32[128,128]{1,0:T(8,128)S(1)} %cholesky.448), custom_call_target="Cholesky" | custom-call | tf_op jit(solution)/shard_map/jit(cholesky)/cholesky | solution.py:49
  467.7 9.8 %custom-call.33 = f32[1,128,128]{1,2,0:T(8,128)S(1)} custom-call(f32[1,128,128]{2,1,0:T(8,128)S(1)} %get-tuple-element.49), custom_call_target="InvertDiagBlocksLowerTriangular" | custom-call | tf_op jit(solution)/shard_map/jit(cholesky)/cholesky | solution.py:49
  478.1 11.7 %cholesky.415 = f32[128,128]{1,0:T(8,128)S(1)} custom-call(f32[128,128]{1,0:T(8,128)S(1)} %convolution_subtract_fusion.9), custom_call_target="Cholesky" | custom-call | tf_op jit(solution)/shard_map/jit(cholesky)/cholesky | solution.py:49
  502.7 39.3 %custom-call.34 = f32[4,128,128]{1,2,0:T(8,128)S(1)} custom-call(f32[4,128,128]{2,1,0:T(8,128)S(1)} %get-tuple-element.19), custom_call_target="InvertDiagBlocksLowerTriangular" | custom-call | tf_op jit(solution)/shard_map/jit(_solve_triangular)/triangular_solve | solution.py:52
  566.3 61.8 %all-reduce.6.cloned.1.call-done = f32[512,1024]{0,1:T(8,128)} async-done(((f32[512,1024]{0,1:T(8,128)}), f32[512,1024]{0,1:T(8,128)}) %all-reduce.6.cloned.1.call-update) | async-done | bytes 2097168 | tf_op jit(solution)/shard_map/psum | solution.py:12
  628.2 18.4 %subtract_select_fusion = f32[2048,1024]{0,1:T(8,128)} fusion(f32[2048,1024]{0,1:T(8,128)} %copy-done, pred[2048]{0:T(1024)(128)(4,1)S(1)} %broadcast_compare_fusion.1, pred[1024]{0:T(1024)(128)(4,1)S(1)} %fusion.86, f32[512,2048]{1,0:T(8,128)} %maximum_select_fusion.1, f32[512,1024]{0,1:T(8,128)} %all-reduce.6.cloned.1.call-done), kind=kOutput, calls=%fused_computation.6 | convolution fusion | flops 12891193344 | bytes 23071744 | tf_op jit(solution)/shard_map/dot_general | solution.py:16
  646.5 9.2 %copy.28 = f32[2048,1024]{1,0:T(8,128)} copy(f32[2048,1024]{0,1:T(8,128)} %subtract_select_fusion) | data formatting | bytes 16777216
  (131 shorter events, 129.0 us)
Async XLA Ops:
  7.2 69.7 %all-gather.11.cloned.1.call-start = ((), (), s32[]{:S(2)}) async-start(), calls=%async_computation.4 | async-start | bytes 1056768 | tf_op jit(solution)/shard_map/all_gather | solution.py:46
  8.7 215.4 %all-gather.7.cloned.1.call-start = ((), (), s32[]{:S(2)}) async-start(), calls=%async_computation | async-start | bytes 4456448 | tf_op jit(solution)/shard_map/all_gather | solution.py:51
  19.6 290.6 %all-reduce.4.cloned.1.call-start = ((), (), s32[]{:S(2)}) async-start(), calls=%async_computation.1 | async-start | bytes 4194304 | tf_op jit(solution)/shard_map/psum | solution.py:12
  224.1 5.7 copy-start.1
  246.5 148.0 %all-gather.13.cloned.1.call-start = ((), (), s32[]{:S(2)}) async-start(), calls=%async_computation.5 | async-start | bytes 1056768 | tf_op jit(solution)/shard_map/all_gather | solution.py:46
  327.2 3.4 copy-start
  331.5 210.6 %all-gather.9.cloned.1.call-start = ((), (), s32[]{:S(2)}) async-start(), calls=%async_computation.2 | async-start | bytes 4456448 | tf_op jit(solution)/shard_map/all_gather | solution.py:51
  333.2 295.0 %all-reduce.6.cloned.1.call-start = ((), (), s32[]{:S(2)}) async-start(), calls=%async_computation.3 | async-start | bytes 4194304 | tf_op jit(solution)/shard_map/psum | solution.py:12
  542.0 5.7 copy-start.2
Sparse Core Ops, SparseCore 0:
  10.8 65.9 all-gather.10
  79.5 49.2 all-gather.6
  246.6 63.5 all-reduce.3
  331.6 62.9 all-gather.12
  397.1 49.4 all-gather.8
  564.5 63.6 all-reduce.5
where the time goes:
time: 668 us; the launch traced here: 663 us
  other arithmetic  258 us (39%)
  waiting for transfers between devices  244 us (37%)
  local copies, waits for them, and re-layouts  78.7 us (12%)
  matrix products  61.3 us (9%)
  between operations  19.7 us (3%)
    another operation x29, other arithmetic, local(): lower_fac = jnp.linalg.cholesky(blocks)  158 us
    psum x2, waiting for transfers between devices, from_root(): return lax.psum(kept, axis)  125 us
    all_gather x2, waiting for transfers between devices, local(): blocks = lax.all_gather(flat_block, ('row', 'col'), axis=0, tiled=True)  118 us
    another operation x5, other arithmetic, local(): jax.scipy.linalg.solve_triangular(lower_fac, gathered, lower=True)  78.9 us
    dot_general x2, matrix products, outer_update(): lax.dot_general(left_fac, right_fac, (((0,), (0,)), ((), ())), precision=...  35.4 us
    unnamed x10, local copies, waits for them, and re-layouts  23.1 us
    another operation x14, matrix products, local(): jax.scipy.linalg.solve_triangular(lower_fac, gathered, lower=True)  22.2 us
    another operation x27, local copies, waits for them, and re-layouts, local(): jax.scipy.linalg.solve_triangular(lower_fac, gathered, lower=True)  15.5 us
  transfers between devices with their start and end apart: 6, of which 4 were waited for; matrix products, arithmetic and copies ran while one was open for 46% of the time, Pallas kernels for 0%

commit v1 on v0

--- a/solution.py
+++ b/solution.py
@@ -9,7 +9,7 @@
 
 def from_root(value, axis, source):
     kept = jnp.where(lax.axis_index(axis) == source, value, 0).astype(value.dtype)
-    return lax.psum(kept, axis)
+    return jnp.sum(lax.all_gather(kept, axis), axis=0)
 
 
 def outer_update(left_fac, right_fac):

time: 668 us -> 727 us (1.088)
  waiting for transfers between devices: 244 us -> 283 us
  other arithmetic: 258 us -> 272 us
    all_gather x0 -> x2, waiting for transfers between devices: none -> 164 us  [from_root(): return jnp.sum(lax.all_gather(kept, axis), axis=0)]
    psum x2 -> x0, waiting for transfers between devices: 125 us -> none  [from_root(): return lax.psum(kept, axis)]
    unnamed x0 -> x2, other arithmetic: none -> 15.9 us
  transfers between devices with their start and end apart: 6 -> 6, of which waited for: 4 -> 4; matrix products, arithmetic and copies ran while one was open for 46% -> 42% of each run, Pallas kernels for 0% -> 0%
where the time goes in v1:
time: 727 us; the launch traced here: 720 us
  waiting for transfers between devices  283 us (39%)
  other arithmetic  272 us (37%)
  local copies, waits for them, and re-layouts  83.6 us (11%)
  matrix products  60.6 us (8%)
  between operations  20.3 us (3%)
    all_gather x2, waiting for transfers between devices, from_root(): return jnp.sum(lax.all_gather(kept, axis), axis=0)  164 us
    another operation x29, other arithmetic, local(): lower_fac = jnp.linalg.cholesky(blocks)  158 us
    all_gather x2, waiting for transfers between devices, local(): blocks = lax.all_gather(flat_block, ('row', 'col'), axis=0, tiled=True)  119 us
    another operation x5, other arithmetic, local(): jax.scipy.linalg.solve_triangular(lower_fac, gathered, lower=True)  78.9 us
    dot_general x2, matrix products, outer_update(): lax.dot_general(left_fac, right_fac, (((0,), (0,)), ((), ())), precision=...  34.6 us
    unnamed x10, local copies, waits for them, and re-layouts  23.1 us
    another operation x14, matrix products, local(): jax.scipy.linalg.solve_triangular(lower_fac, gathered, lower=True)  22.2 us
    another operation x27, local copies, waits for them, and re-layouts, local(): jax.scipy.linalg.solve_triangular(lower_fac, gathered, lower=True)  16.2 us
  transfers between devices with their start and end apart: 6, of which 4 were waited for; matrix products, arithmetic and copies ran while one was open for 42% of the time, Pallas kernels for 0%

profile of v1, /device:TPU:0, one launch (start us, length us, event | category | flops | bytes accessed | tf_op | source)
XLA Modules:
  0.0 720.1 jit_solution(1605004012382470696)
XLA Ops:
  8.7 9.1 %copy.24 = f32[2048,1024]{0,1:T(8,128)} copy(f32[2048,1024]{1,0:T(8,128)} %param.4) | data formatting | bytes 16777216 | tf_op args[0]
  19.7 57.2 %all-gather.17.cloned.1.call-done = f32[128,1,2048]{2,1,0:T(1,128)} async-done(((f32[1,1,2048]{2,1,0:T(1,128)}), f32[128,1,2048]{2,1,0:T(1,128)}) %all-gather.17.cloned.1.call-update) | async-done | bytes 1048592 | tf_op jit(solution)/shard_map/all_gather | solution.py:46
  93.3 11.7 %cholesky.286 = f32[128,128]{1,0:T(8,128)S(1)} custom-call(f32[128,128]{1,0:T(8,128)S(1)} %cholesky.426), custom_call_target="Cholesky" | custom-call | tf_op jit(solution)/shard_map/jit(cholesky)/cholesky | solution.py:49
  105.0 9.8 %custom-call.27 = f32[1,128,128]{1,2,0:T(8,128)S(1)} custom-call(f32[1,128,128]{2,1,0:T(8,128)S(1)} %get-tuple-element.65), custom_call_target="InvertDiagBlocksLowerTriangular" | custom-call | tf_op jit(solution)/shard_map/jit(cholesky)/cholesky | solution.py:49
  115.6 11.7 %cholesky.305 = f32[128,128]{1,0:T(8,128)S(1)} custom-call(f32[128,128]{1,0:T(8,128)S(1)} %cholesky.430), custom_call_target="Cholesky" | custom-call | tf_op jit(solution)/shard_map/jit(cholesky)/cholesky | solution.py:49
  127.4 10.2 %custom-call.28 = f32[1,128,128]{1,2,0:T(8,128)S(1)} custom-call(f32[1,128,128]{2,1,0:T(8,128)S(1)} %get-tuple-element.62), custom_call_target="InvertDiagBlocksLowerTriangular" | custom-call | tf_op jit(solution)/shard_map/jit(cholesky)/cholesky | solution.py:49
  138.2 11.7 %cholesky.326 = f32[128,128]{1,0:T(8,128)S(1)} custom-call(f32[128,128]{1,0:T(8,128)S(1)} %cholesky.435), custom_call_target="Cholesky" | custom-call | tf_op jit(solution)/shard_map/jit(cholesky)/cholesky | solution.py:49
  150.0 9.8 %custom-call.29 = f32[1,128,128]{1,2,0:T(8,128)S(1)} custom-call(f32[1,128,128]{2,1,0:T(8,128)S(1)} %get-tuple-element.59), custom_call_target="InvertDiagBlocksLowerTriangular" | custom-call | tf_op jit(solution)/shard_map/jit(cholesky)/cholesky | solution.py:49
  160.4 11.7 %cholesky.343 = f32[128,128]{1,0:T(8,128)S(1)} custom-call(f32[128,128]{1,0:T(8,128)S(1)} %convolution_subtract_fusion.10), custom_call_target="Cholesky" | custom-call | tf_op jit(solution)/shard_map/jit(cholesky)/cholesky | solution.py:49
  184.8 39.3 %custom-call.30 = f32[4,128,128]{1,2,0:T(8,128)S(1)} custom-call(f32[4,128,128]{2,1,0:T(8,128)S(1)} %get-tuple-element.18), custom_call_target="InvertDiagBlocksLowerTriangular" | custom-call | tf_op jit(solution)/shard_map/jit(_solve_triangular)/triangular_solve | solution.py:52
  247.2 82.6 %all-gather.11.cloned.1.call-done = f32[8,512,1024]{2,1,0:T(8,128)} async-done(((f32[1,512,1024]{2,1,0:T(8,128)}), f32[8,512,1024]{2,1,0:T(8,128)}) %all-gather.11.cloned.1.call-update) | async-done | bytes 16777232 | tf_op jit(solution)/shard_map/all_gather | solution.py:12
  337.8 16.0 %convolution_subtract_fusion = f32[2048,1024]{0,1:T(8,128)S(1)} fusion(f32[2048,1024]{0,1:T(8,128)} %copy.24, f32[512,2048]{1,0:T(8,128)} %maximum_select_fusion, f32[512,1024]{1,0:T(8,128)S(1)} %reduce_sum.18), kind=kOutput, calls=%fused_computation.9 | convolution fusion | flops 12886999040 | bytes 23068672 | tf_op jit(solution)/shard_map/dot_general | solution.py:16
  359.9 62.3 %all-gather.19.cloned.1.call-done = f32[128,1,2048]{2,1,0:T(1,128)} async-done(((f32[1,1,2048]{2,1,0:T(1,128)}), f32[128,1,2048]{2,1,0:T(1,128)}) %all-gather.19.cloned.1.call-update) | async-done | bytes 1048592 | tf_op jit(solution)/shard_map/all_gather | solution.py:46
  438.8 11.7 %cholesky.358 = f32[128,128]{1,0:T(8,128)S(1)} custom-call(f32[128,128]{1,0:T(8,128)S(1)} %cholesky.439), custom_call_target="Cholesky" | custom-call | tf_op jit(solution)/shard_map/jit(cholesky)/cholesky | solution.py:49
  450.7 9.8 %custom-call.31 = f32[1,128,128]{1,2,0:T(8,128)S(1)} custom-call(f32[1,128,128]{2,1,0:T(8,128)S(1)} %get-tuple-element.55), custom_call_target="InvertDiagBlocksLowerTriangular" | custom-call | tf_op jit(solution)/shard_map/jit(cholesky)/cholesky | solution.py:49
  461.2 11.7 %cholesky.377 = f32[128,128]{1,0:T(8,128)S(1)} custom-call(f32[128,128]{1,0:T(8,128)S(1)} %cholesky.443), custom_call_target="Cholesky" | custom-call | tf_op jit(solution)/shard_map/jit(cholesky)/cholesky | solution.py:49
  472.9 10.0 %custom-call.32 = f32[1,128,128]{1,2,0:T(8,128)S(1)} custom-call(f32[1,128,128]{2,1,0:T(8,128)S(1)} %get-tuple-element.52), custom_call_target="InvertDiagBlocksLowerTriangular" | custom-call | tf_op jit(solution)/shard_map/jit(cholesky)/cholesky | solution.py:49
  483.6 11.7 %cholesky.398 = f32[128,128]{1,0:T(8,128)S(1)} custom-call(f32[128,128]{1,0:T(8,128)S(1)} %cholesky.448), custom_call_target="Cholesky" | custom-call | tf_op jit(solution)/shard_map/jit(cholesky)/cholesky | solution.py:49
  495.3 9.8 %custom-call.33 = f32[1,128,128]{1,2,0:T(8,128)S(1)} custom-call(f32[1,128,128]{2,1,0:T(8,128)S(1)} %get-tuple-element.49), custom_call_target="InvertDiagBlocksLowerTriangular" | custom-call | tf_op jit(solution)/shard_map/jit(cholesky)/cholesky | solution.py:49
  505.8 11.7 %cholesky.415 = f32[128,128]{1,0:T(8,128)S(1)} custom-call(f32[128,128]{1,0:T(8,128)S(1)} %convolution_subtract_fusion.9), custom_call_target="Cholesky" | custom-call | tf_op jit(solution)/shard_map/jit(cholesky)/cholesky | solution.py:49
  531.6 39.3 %custom-call.34 = f32[4,128,128]{1,2,0:T(8,128)S(1)} custom-call(f32[4,128,128]{2,1,0:T(8,128)S(1)} %get-tuple-element.19), custom_call_target="InvertDiagBlocksLowerTriangular" | custom-call | tf_op jit(solution)/shard_map/jit(_solve_triangular)/triangular_solve | solution.py:52
  596.0 81.0 %all-gather.15.cloned.1.call-done = f32[8,512,1024]{2,1,0:T(8,128)} async-done(((f32[1,512,1024]{2,1,0:T(8,128)}), f32[8,512,1024]{2,1,0:T(8,128)}) %all-gather.15.cloned.1.call-update) | async-done | bytes 16777232 | tf_op jit(solution)/shard_map/all_gather | solution.py:12
  685.0 18.6 %subtract_select_fusion = f32[2048,1024]{0,1:T(8,128)} fusion(f32[2048,1024]{0,1:T(8,128)} %copy-done, pred[2048]{0:T(1024)(128)(4,1)S(1)} %broadcast_compare_fusion.1, pred[1024]{0:T(1024)(128)(4,1)S(1)} %fusion.86, f32[512,2048]{1,0:T(8,128)} %maximum_select_fusion.1, f32[512,1024]{1,0:T(8,128)S(1)} %reduce_sum.19), kind=kOutput, calls=%fused_computation.6 | convolution fusion | flops 12891193344 | bytes 23071744 | tf_op jit(solution)/shard_map/dot_general | solution.py:16
  703.6 9.2 %copy.32 = f32[2048,1024]{1,0:T(8,128)} copy(f32[2048,1024]{0,1:T(8,128)} %subtract_select_fusion) | data formatting | bytes 16777216
  (135 shorter events, 148.0 us)
Async XLA Ops:
  7.2 69.7 %all-gather.17.cloned.1.call-start = ((), (), s32[]{:S(2)}) async-start(), calls=%async_computation.4 | async-start | bytes 1056768 | tf_op jit(solution)/shard_map/all_gather | solution.py:46
  8.7 215.4 %all-gather.9.cloned.1.call-start = ((), (), s32[]{:S(2)}) async-start(), calls=%async_computation | async-start | bytes 4456448 | tf_op jit(solution)/shard_map/all_gather | solution.py:51
  19.6 310.3 %all-gather.11.cloned.1.call-start = ((), (), s32[]{:S(2)}) async-start(), calls=%async_computation.1 | async-start | bytes 18874368 | tf_op jit(solution)/shard_map/all_gather | solution.py:12
  224.1 5.7 copy-start.1
  246.9 175.3 %all-gather.19.cloned.1.call-start = ((), (), s32[]{:S(2)}) async-start(), calls=%async_computation.5 | async-start | bytes 1056768 | tf_op jit(solution)/shard_map/all_gather | solution.py:46
  353.8 3.4 copy-start
  358.1 212.9 %all-gather.13.cloned.1.call-start = ((), (), s32[]{:S(2)}) async-start(), calls=%async_computation.2 | async-start | bytes 4456448 | tf_op jit(solution)/shard_map/all_gather | solution.py:51
  359.8 317.2 %all-gather.15.cloned.1.call-start = ((), (), s32[]{:S(2)}) async-start(), calls=%async_computation.3 | async-start | bytes 18874368 | tf_op jit(solution)/shard_map/all_gather | solution.py:12
  571.0 5.7 copy-start.2
Sparse Core Ops, SparseCore 0:
  10.8 65.9 all-gather.16
  79.5 49.3 all-gather.8
  247.0 82.7 all-gather.10
  358.2 63.9 all-gather.18
  424.8 49.0 all-gather.12
  594.2 82.7 all-gather.14
